TPU v7x, 128 devices: a whole 4x4x4 slice. The times are simulated.
128 devices in a mesh: rows: 8 (over z, x_lo), cols: 16 (over y, x_hi, core).
Axes of the slice: x: 4 (x_hi: 2, x_lo: 2; x = x_hi * 2 + x_lo), y: 4, z: 4, core: 2. Of those that a mesh axis runs over, the one named last changes fastest.
Arguments:
- global_in: bfloat16 [16, 64, 1024], P('rows', None, 'cols'), may hold values from -6 to 6
- global_first: bfloat16 [3, 3, 1024, 1024], P(None, None, None, 'cols'), may hold values from -0.0625 to 0.0625
- global_second: bfloat16 [3, 3, 1024, 1024], P(None, None, None, 'cols'), may hold values from -0.0625 to 0.0625
- project_weight: bfloat16 [1024, 128], replicated, may hold values from -0.1875 to 0.1875
- enhancer_input: bfloat16 [256, 1024, 128], P('rows', 'cols'), may hold values from -6 to 6
- instance_map: int32 [256, 1024], P('rows', 'cols'), may hold values from 0 to 255, as said below
- encoder_features: float32 [16, 256, 1024], P(None, 'rows', 'cols'), may hold values from -5 to 5
- instance_weight: float32 [16, 128], replicated, may hold values from -4 to 4
- enhancer_first: bfloat16 [3, 3, 128, 128], replicated, may hold values from -0.1875 to 0.1875
- enhancer_second: bfloat16 [3, 3, 128, 128], replicated, may hold values from -0.1875 to 0.1875
- output_cotangent: bfloat16 [256, 1024, 128], P('rows', 'cols'), may hold values from -6 to 6
Outputs:
- enhanced: bfloat16 [256, 1024, 128], P('rows', 'cols')
- gradient_first: float32 [3, 3, 128, 128], replicated
- gradient_second: float32 [3, 3, 128, 128], replicated
- global_gradient: float32 [16, 64, 128], P('rows', 'cols')
Inputs may be any that keep to these rules, and one draw needn't show every extreme that they name: `instance_map`: constant on each aligned 16 x 16 block of fine pixels.
All inputs are finite; a program needn't handle non-finite values.
Results may differ from a plain program's by a relative error of at most 0.0075.
Values may be sent and summed in bfloat16 or wider, within the bound.
A program may use at most 64 MiB of HBM per device.

v0:
```python
import math

import jax
import jax.numpy as jnp
from jax import lax
from jax.sharding import PartitionSpec as P

INSTANCES = 256
UPSCALE = 16


norm_eps = 1e-05


def padded_2(array, sides, width):
    for axis, dim in sides:
        devices, length = (lax.axis_size(axis), array.shape[dim])
        up = [(i, (i + 1) % devices) for i in range(devices - 1)]
        down = [(j, i) for i, j in up]
        last = lax.slice_in_dim(array, length - width, length, axis=dim)
        initial = lax.slice_in_dim(array, 0, width, axis=dim)
        before = lax.ppermute(last, axis, up)
        after = lax.ppermute(initial, axis, down)
        array = jnp.concatenate([before, array, after], axis=dim)
    return array


def conv_taps(padded, weight, row_count, col_count):
    summed = jnp.zeros((row_count * col_count, weight.shape[3]), jnp.float32)
    for tap_row in range(3):
        for tap_col in range(3):
            window = padded[tap_row : tap_row + row_count, tap_col : tap_col + col_count]
            summed = summed + jnp.dot(
                window.reshape(row_count * col_count, window.shape[2]),
                weight[tap_row, tap_col],
                preferred_element_type=jnp.float32,
            )
    return summed


def back_taps(padded, weight, row_count, col_count):
    summed = jnp.zeros((row_count * col_count, weight.shape[2]), jnp.float32)
    for tap_row in range(3):
        for tap_col in range(3):
            window = padded[
                2 - tap_row : 2 - tap_row + row_count, 2 - tap_col : 2 - tap_col + col_count
            ]
            summed = summed + jnp.dot(
                window.reshape(row_count * col_count, window.shape[2]),
                weight[tap_row, tap_col].T,
                preferred_element_type=jnp.float32,
            )
    return summed


def weight_taps(padded, gradient, row_count, col_count):
    flattened = gradient.reshape(row_count * col_count, gradient.shape[2])
    stacked = []
    for tap_row in range(3):
        line = []
        for tap_col in range(3):
            window = padded[tap_row : tap_row + row_count, tap_col : tap_col + col_count]
            line.append(
                lax.dot_general(
                    window.reshape(row_count * col_count, window.shape[2]),
                    flattened,
                    (((0,), (0,)), ((), ())),
                    preferred_element_type=jnp.float32,
                )
            )
        stacked.append(jnp.stack(line))
    return jnp.stack(stacked)


def band_conv(band_field, weight):
    band_rows, band_cols, width_share = band_field.shape
    gathered = lax.all_gather(band_field, "cols", axis=2, tiled=True)
    rimmed = padded_2(gathered, (("rows", 0),), 1)
    rimmed = jnp.pad(rimmed, ((0, 0), (1, 1), (0, 0)))
    result = conv_taps(rimmed, weight, band_rows, band_cols)
    return result


def tile_conv(field, weight):
    padded = padded_2(field, (("rows", 0), ("cols", 1)), 1)
    return (padded, conv_taps(padded, weight, field.shape[0], field.shape[1]))


def grad_halo(field):
    return padded_2(field, (("rows", 0), ("cols", 1)), 1)


def per_device(
    global_in,
    global_first,
    global_second,
    project_weight,
    enhancer_input,
    instance_map,
    encoder_features,
    instance_weight,
    enhancer_first,
    enhancer_second,
    output_cotangent,
):
    band_rows, band_cols, width_share = global_in.shape
    tile_rows, tile_cols, local_width = enhancer_input.shape
    first_raw = band_conv(global_in, global_first)
    band_sum, band_square = lax.psum(
        (jnp.sum(first_raw, 0), jnp.sum(first_raw * first_raw, 0)), "rows"
    )
    band_total = band_rows * band_cols * lax.axis_size("rows")
    band_mean = band_sum / band_total
    band_var = band_square / band_total - band_mean * band_mean
    normed = (first_raw - band_mean) * lax.rsqrt(band_var + norm_eps)
    hidden = (
        jnp.maximum(normed, 0.0).astype(jnp.bfloat16).reshape(band_rows, band_cols, width_share)
    )
    second_raw = band_conv(hidden, global_second)
    global_out = (
        (global_in.astype(jnp.float32).reshape(-1, width_share) + second_raw)
        .astype(jnp.bfloat16)
        .reshape(band_rows, band_cols, width_share)
    )
    weight_rows = lax.dynamic_slice_in_dim(
        project_weight, lax.axis_index("cols") * width_share, width_share, 0
    )
    reduced = lax.psum_scatter(
        jnp.einsum("bwc,cd->wbd", global_out, weight_rows, preferred_element_type=jnp.float32),
        "cols",
        scatter_dimension=0,
        tiled=True,
    )
    coarse = jnp.transpose(reduced, (1, 0, 2)).astype(jnp.bfloat16)
    block_rows = tile_rows // UPSCALE
    block_cols = tile_cols // UPSCALE
    block_labels = instance_map[::UPSCALE, ::UPSCALE].reshape(-1)
    one_hot = (block_labels[:, None] == jnp.arange(INSTANCES, dtype=jnp.int32)[None, :]).astype(
        jnp.float32
    )
    encoder_width = encoder_features.shape[0]
    block_sums = (
        encoder_features.reshape(encoder_width, block_rows, UPSCALE, block_cols, UPSCALE)
        .sum(axis=(2, 4))
        .reshape(encoder_width, -1)
    )
    feature_sums = jnp.dot(block_sums, one_hot, precision=lax.Precision.HIGHEST)
    member_counts = jnp.sum(one_hot, 0) * float(UPSCALE * UPSCALE)
    feature_sums, member_counts = lax.psum((feature_sums, member_counts), ("rows", "cols"))
    averages = feature_sums / jnp.maximum(member_counts, 1.0)
    lookup = jnp.dot(averages.T, instance_weight, precision=lax.Precision.HIGHEST)
    pooled_blocks = jnp.dot(one_hot, lookup, precision=lax.Precision.HIGHEST).reshape(
        block_rows, block_cols, local_width
    )
    block_terms = coarse.astype(jnp.float32) + pooled_blocks
    upsampled = jnp.repeat(jnp.repeat(block_terms, UPSCALE, 0), UPSCALE, 1)
    mixed = (enhancer_input.astype(jnp.float32) + upsampled).astype(jnp.bfloat16)
    mixed_padded, first_act = tile_conv(mixed, enhancer_first)
    pixel_total = tile_rows * tile_cols * lax.axis_size("rows") * lax.axis_size("cols")
    act_sum, act_square = lax.psum(
        (jnp.sum(first_act, 0), jnp.sum(first_act * first_act, 0)), ("rows", "cols")
    )
    act_mean = act_sum / pixel_total
    inverse_dev = lax.rsqrt(act_square / pixel_total - act_mean * act_mean + norm_eps)
    normed_act = (first_act - act_mean) * inverse_dev
    activated = (
        jax.nn.silu(normed_act).astype(jnp.bfloat16).reshape(tile_rows, tile_cols, local_width)
    )
    active_padded, second_act = tile_conv(activated, enhancer_second)
    enhanced = (
        (mixed.astype(jnp.float32).reshape(-1, local_width) + second_act)
        .astype(jnp.bfloat16)
        .reshape(tile_rows, tile_cols, local_width)
    )
    cotangent_padded = grad_halo(output_cotangent)
    second_local = weight_taps(active_padded, output_cotangent, tile_rows, tile_cols)
    act_grad = back_taps(cotangent_padded, enhancer_second, tile_rows, tile_cols)
    gate_value = jax.nn.sigmoid(normed_act)
    normed_grad = act_grad * gate_value * (1.0 + normed_act * (1.0 - gate_value))
    grad_sum, cross_sum = lax.psum(
        (jnp.sum(normed_grad, 0), jnp.sum(normed_grad * normed_act, 0)), ("rows", "cols")
    )
    first_grad = (
        (
            inverse_dev
            * (normed_grad - grad_sum / pixel_total - normed_act * (cross_sum / pixel_total))
        )
        .astype(jnp.bfloat16)
        .reshape(tile_rows, tile_cols, local_width)
    )
    first_local = weight_taps(mixed_padded, first_grad, tile_rows, tile_cols)
    first_padded = grad_halo(first_grad)
    mixed_grad = output_cotangent.astype(jnp.float32).reshape(-1, local_width) + back_taps(
        first_padded, enhancer_first, tile_rows, tile_cols
    )
    global_gradient = (
        mixed_grad.reshape(block_rows, UPSCALE, block_cols, UPSCALE, local_width).sum(axis=(1, 3))
        / UPSCALE
    )
    first_total, second_total = lax.psum((first_local, second_local), ("rows", "cols"))
    rescale = 1.0 / math.sqrt(pixel_total)
    return (enhanced, first_total * rescale, second_total * rescale, global_gradient)


def solution(mesh):
    return jax.shard_map(
        per_device,
        mesh=mesh,
        in_specs=(
            P("rows", None, "cols"),
            P(None, None, None, "cols"),
            P(None, None, None, "cols"),
            P(),
            P("rows", "cols", None),
            P("rows", "cols"),
            P(None, "rows", "cols"),
            P(),
            P(),
            P(),
            P("rows", "cols", None),
        ),
        out_specs=(P("rows", "cols", None), P(), P(), P("rows", "cols", None)),
        check_vma=False,
    )
```

profile of v0, /device:TPU:1, one launch (start us, length us, event | category | flops | bytes accessed | tf_op | source)
XLA Modules:
  0.0 623.2 jit_solution(580691706944969219)
XLA Ops:
  8.2 28.1 %all_gather.6 = bf16[2,64,1024]{1,0,2:T(2,128)(2,1)S(1)} all-gather(bf16[2,64,64]{1,0,2:T(2,128)(2,1)S(1)} %copy.47), channel_id=1, replica_groups=mesh['rows'=8,'cols'=16] {'cols'}, dimensions={2}, use_global_device_ids=true | all-gather | bytes 278528 | tf_op jit(solution)/shard_map/all_gather | solution.py:77
  37.4 2.2 collective-permute-start
  40.9 5.0 collective-permute-start.12
  49.3 68.6 %all-reduce.5 = (f32[16,256]{1,0:T(8,128)S(1)}, f32[256]{0:T(256)S(1)}) all-reduce(f32[16,256]{1,0:T(8,128)S(1)} %fusion.158, f32[256]{0:T(256)S(1)} %broadcast_multiply_fusion.3), channel_id=1, replica_groups=mesh['rows'=8,'cols'=16] {'rows','cols'}, use_global_device_ids=true, to_apply=%region_6.7 | all-reduce | flops 4352 | bytes 34816 | tf_op jit(solution)/shard_map/psum | solution.py:149
  120.9 3.0 collective-permute-start.14
  123.9 4.1 collective-permute-start.15
  137.2 13.7 %all-reduce.7 = (f32[64]{0:T(128)S(1)}, f32[64]{0:T(128)S(1)}) all-reduce(f32[64]{0:T(128)S(1)} %get-tuple-element.9, f32[64]{0:T(128)S(1)} %get-tuple-element.8), channel_id=1, replica_groups=mesh['rows'=8,'cols'=16] {'rows'}, use_global_device_ids=true, to_apply=%region_3.4 | all-reduce | flops 128 | bytes 1024 | tf_op jit(solution)/shard_map/psum | solution.py:109
  151.2 30.2 %all_gather.7 = bf16[2,64,1024]{1,0,2:T(2,128)(2,1)} all-gather(bf16[2,64,64]{1,0,2:T(2,128)(2,1)S(1)} %reshape.252), channel_id=1, replica_groups=mesh['rows'=8,'cols'=16] {'cols'}, dimensions={2}, use_global_device_ids=true | all-gather | bytes 278528 | tf_op jit(solution)/shard_map/all_gather | solution.py:77
  185.3 2.0 convolution_add_fusion.8
  187.3 3.9 collective-permute-done.3
  195.0 60.8 %all-reduce.2 = bf16[64,2,128]{2,0,1:T(8,128)(2,1)S(1)} all-reduce(f32[64,2,128]{2,0,1:T(8,128)S(1)} %convolution_bitcast_fusion.18), channel_id=2, replica_groups=mesh['rows'=8,'cols'=16] {'cols'}, use_global_device_ids=true, to_apply=%region_4.5.clone | all-reduce | flops 16384 | bytes 98304
  256.0 2.5 collective-permute-start.4
  263.0 7.1 %collective-permute-start.6 = (bf16[34,1,128]{2,1,0:T(2,128)(2,1)S(1)}, bf16[34,1,128]{2,1,0:T(2,128)(2,1)S(1)}, u32[]{:S(2)}, u32[]{:S(2)}) collective-permute-start(bf16[34,1,128]{2,1,0:T(2,128)(2,1)S(1)} %get-tuple-element.73), channel_id=1, source_target_pairs={{0,1},{1,2},{2,3},{3,4},{4,5},{5,6},{6,7},{7,8},{8,9},{9,10},{10,1... | collective-permute-start | bytes 26120 | tf_op jit(solution)/shard_map/ppermute | solution.py:22
  270.1 3.6 collective-permute-start.7
  274.1 2.6 collective-permute-done.7
  281.4 61.8 %all-reduce.4 = (f32[128]{0:T(128)S(1)}, f32[128]{0:T(128)S(1)}) all-reduce(f32[128]{0:T(128)S(1)} %get-tuple-element.7, f32[128]{0:T(128)S(1)} %get-tuple-element.6), channel_id=1, replica_groups=mesh['rows'=8,'cols'=16] {'rows','cols'}, use_global_device_ids=true, to_apply=%region_12.13 | all-reduce | flops 256 | bytes 2048 | tf_op jit(solution)/shard_map/psum | solution.py:160
  343.2 3.8 fusion.170
  347.0 63.3 %all-reduce.3 = (f32[128]{0:T(128)S(1)}, f32[128]{0:T(128)S(1)}) all-reduce(f32[128]{0:T(128)S(1)} %get-tuple-element.5, f32[128]{0:T(128)S(1)} %get-tuple-element.4), channel_id=1, replica_groups=mesh['rows'=8,'cols'=16] {'rows','cols'}, use_global_device_ids=true, to_apply=%region_16.17 | all-reduce | flops 256 | bytes 2048 | tf_op jit(solution)/shard_map/psum | solution.py:180
  420.1 4.0 collective-permute-start.8
  426.8 3.4 collective-permute-start.18
  430.2 4.0 collective-permute-start.19
  434.3 2.4 collective-permute-start.10
  436.7 2.1 collective-permute-start.11
  469.8 143.7 %all-reduce.10.cloned.1.call-done = (f32[3,3,128,128]{3,2,1,0:T(8,128)}, f32[3,3,128,128]{3,2,1,0:T(8,128)}) async-done(((f32[3,3,128,128]{3,2,1,0:T(8,128)}, f32[3,3,128,128]{3,2,1,0:T(8,128)}), (f32[3,3,128,128]{3,2,1,0:T(8,128)}, f32[3,3,128,128]{3,2,1,0:T(8,128)})) %all-reduce.10.cloned.1.call-update) | async-done | bytes 1179664 | tf_op jit(solution)/shard_map/psum | solution.py:200
  (252 shorter events, 81.2 us)
Async XLA Ops:
  7.2 187.7 %copy-start = (bf16[1024,128]{1,0:T(8,128)(2,1)S(1)}, bf16[1024,128]{1,0:T(8,128)(2,1)}, u32[]{:S(2)}) copy-start(bf16[1024,128]{1,0:T(8,128)(2,1)} %param.14) | copy-start | bytes 786436
  7.2 606.3 %all-reduce.10.cloned.1.call-start = ((), (), s32[]{:S(2)}) async-start(), calls=%async_computation | async-start | bytes 2359296 | tf_op jit(solution)/shard_map/psum | solution.py:200
  37.4 95.7 %collective-permute-start = (bf16[1,64,1024]{2,1,0:T(8,128)(2,1)}, bf16[1,64,1024]{2,1,0:T(8,128)(2,1)S(1)}, u32[]{:S(2)}, u32[]{:S(2)}) collective-permute-start(bf16[1,64,1024]{2,1,0:T(8,128)(2,1)} %get-tuple-element.98), channel_id=1, source_target_pairs={{0,16},{16,32},{32,48},{48,64},{64,80},{80,96},{96,112},{1,17},{17... | collective-permute-start | bytes 393224 | tf_op jit(solution)/shard_map/ppermute | solution.py:22
  39.6 93.5 %collective-permute-start.1 = (bf16[1,64,1024]{2,1,0:T(8,128)(2,1)}, bf16[1,64,1024]{2,1,0:T(8,128)(2,1)S(1)}, u32[]{:S(2)}, u32[]{:S(2)}) collective-permute-start(bf16[1,64,1024]{2,1,0:T(8,128)(2,1)} %get-tuple-element.99), channel_id=1, source_target_pairs={{16,0},{32,16},{48,32},{64,48},{80,64},{96,80},{112,96},{17,1},{33... | collective-permute-start | bytes 393224 | tf_op jit(solution)/shard_map/ppermute | solution.py:23
  40.9 79.6 %collective-permute-start.12 = (bf16[1,64,128]{2,1,0:T(8,128)(2,1)S(1)}, bf16[1,64,128]{2,1,0:T(8,128)(2,1)S(1)}, u32[]{:S(2)}, u32[]{:S(2)}) collective-permute-start(bf16[1,64,128]{2,1,0:T(8,128)(2,1)S(1)} %get-tuple-element.83), channel_id=1, source_target_pairs={{0,16},{16,32},{32,48},{48,64},{64,80},{80,96},{96,112},{1,17},{17... | collective-permute-start | bytes 49160 | tf_op jit(solution)/shard_map/ppermute | solution.py:22
  45.9 74.6 %collective-permute-start.13 = (bf16[1,64,128]{2,1,0:T(8,128)(2,1)S(1)}, bf16[1,64,128]{2,1,0:T(8,128)(2,1)S(1)}, u32[]{:S(2)}, u32[]{:S(2)}) collective-permute-start(bf16[1,64,128]{2,1,0:T(8,128)(2,1)S(1)} %get-tuple-element.82), channel_id=1, source_target_pairs={{16,0},{32,16},{48,32},{64,48},{80,64},{96,80},{112,96},{17,1},{33... | collective-permute-start | bytes 49160 | tf_op jit(solution)/shard_map/ppermute | solution.py:23
  48.1 70.4 %copy-start.31 = (bf16[2,64,64]{2,1,0:T(8,128)(2,1)S(1)}, bf16[2,64,64]{2,1,0:T(8,128)(2,1)}, u32[]{:S(2)}) copy-start(bf16[2,64,64]{2,1,0:T(8,128)(2,1)} %param.11) | copy-start | bytes 49156
  48.1 71.1 %copy-start.40 = (u32[128]{0:T(128)S(1)}, u32[128]{0:T(128)}, u32[]{:S(2)}) copy-start(u32[128]{0:T(128)} %constant.47) | copy-start | bytes 1540
  120.9 8.7 %collective-permute-start.14 = (bf16[34,1,128]{2,1,0:T(2,128)(2,1)S(1)}, bf16[34,1,128]{2,1,0:T(2,128)(2,1)S(1)}, u32[]{:S(2)}, u32[]{:S(2)}) collective-permute-start(bf16[34,1,128]{2,1,0:T(2,128)(2,1)S(1)} %get-tuple-element.65), channel_id=1, source_target_pairs={{1,0},{2,1},{3,2},{4,3},{5,4},{6,5},{7,6},{8,7},{9,8},{10,9},{11,1... | collective-permute-start | bytes 26120 | tf_op jit(solution)/shard_map/ppermute | solution.py:23
  123.9 5.8 collective-permute-start.15
  182.7 4.6 collective-permute-start.2
  184.0 7.2 %collective-permute-start.3 = (bf16[1,64,1024]{2,1,0:T(8,128)(2,1)S(1)}, bf16[1,64,1024]{2,1,0:T(8,128)(2,1)S(1)}, u32[]{:S(2)}, u32[]{:S(2)}) collective-permute-start(bf16[1,64,1024]{2,1,0:T(8,128)(2,1)S(1)} %get-tuple-element.95), channel_id=1, source_target_pairs={{16,0},{32,16},{48,32},{64,48},{80,64},{96,80},{112,96},{17,1},{33... | collective-permute-start | bytes 393224 | tf_op jit(solution)/shard_map/ppermute | solution.py:23
  256.0 5.9 collective-permute-start.4
  258.5 4.5 collective-permute-start.5
  263.0 11.1 %collective-permute-start.6 = (bf16[34,1,128]{2,1,0:T(2,128)(2,1)S(1)}, bf16[34,1,128]{2,1,0:T(2,128)(2,1)S(1)}, u32[]{:S(2)}, u32[]{:S(2)}) collective-permute-start(bf16[34,1,128]{2,1,0:T(2,128)(2,1)S(1)} %get-tuple-element.73), channel_id=1, source_target_pairs={{0,1},{1,2},{2,3},{3,4},{4,5},{5,6},{6,7},{7,8},{8,9},{9,10},{10,1... | collective-permute-start | bytes 26120 | tf_op jit(solution)/shard_map/ppermute | solution.py:22
  270.1 6.6 %collective-permute-start.7 = (bf16[34,1,128]{2,1,0:T(2,128)(2,1)S(1)}, bf16[34,1,128]{2,1,0:T(2,128)(2,1)S(1)}, u32[]{:S(2)}, u32[]{:S(2)}) collective-permute-start(bf16[34,1,128]{2,1,0:T(2,128)(2,1)S(1)} %get-tuple-element.74), channel_id=1, source_target_pairs={{1,0},{2,1},{3,2},{4,3},{5,4},{6,5},{7,6},{8,7},{9,8},{10,9},{11,1... | collective-permute-start | bytes 26120 | tf_op jit(solution)/shard_map/ppermute | solution.py:23
  416.9 9.5 %collective-permute-start.16 = (bf16[1,64,128]{2,1,0:T(8,128)(2,1)S(1)}, bf16[1,64,128]{2,1,0:T(8,128)(2,1)S(1)}, u32[]{:S(2)}, u32[]{:S(2)}) collective-permute-start(bf16[1,64,128]{2,1,0:T(8,128)(2,1)S(1)} %get-tuple-element.77), channel_id=1, source_target_pairs={{0,16},{16,32},{32,48},{48,64},{64,80},{80,96},{96,112},{1,17},{17... | collective-permute-start | bytes 49160 | tf_op jit(solution)/shard_map/ppermute | solution.py:22
  418.8 7.6 %collective-permute-start.17 = (bf16[1,64,128]{2,1,0:T(8,128)(2,1)S(1)}, bf16[1,64,128]{2,1,0:T(8,128)(2,1)S(1)}, u32[]{:S(2)}, u32[]{:S(2)}) collective-permute-start(bf16[1,64,128]{2,1,0:T(8,128)(2,1)S(1)} %get-tuple-element.78), channel_id=1, source_target_pairs={{16,0},{32,16},{48,32},{64,48},{80,64},{96,80},{112,96},{17,1},{33... | collective-permute-start | bytes 49160 | tf_op jit(solution)/shard_map/ppermute | solution.py:23
  420.1 14.1 %collective-permute-start.8 = (bf16[1,64,128]{2,1,0:T(8,128)(2,1)S(1)}, bf16[1,64,128]{2,1,0:T(8,128)(2,1)S(1)}, u32[]{:S(2)}, u32[]{:S(2)}) collective-permute-start(bf16[1,64,128]{2,1,0:T(8,128)(2,1)S(1)} %get-tuple-element.86), channel_id=1, source_target_pairs={{0,16},{16,32},{32,48},{48,64},{64,80},{80,96},{96,112},{1,17},{17... | collective-permute-start | bytes 49160 | tf_op jit(solution)/shard_map/ppermute | solution.py:22
  424.1 10.1 %collective-permute-start.9 = (bf16[1,64,128]{2,1,0:T(8,128)(2,1)S(1)}, bf16[1,64,128]{2,1,0:T(8,128)(2,1)S(1)}, u32[]{:S(2)}, u32[]{:S(2)}) collective-permute-start(bf16[1,64,128]{2,1,0:T(8,128)(2,1)S(1)} %get-tuple-element.87), channel_id=1, source_target_pairs={{16,0},{32,16},{48,32},{64,48},{80,64},{96,80},{112,96},{17,1},{33... | collective-permute-start | bytes 49160 | tf_op jit(solution)/shard_map/ppermute | solution.py:23
  426.8 25.3 %collective-permute-start.18 = (bf16[34,1,128]{2,1,0:T(2,128)(2,1)S(1)}, bf16[34,1,128]{2,1,0:T(2,128)(2,1)S(1)}, u32[]{:S(2)}, u32[]{:S(2)}) collective-permute-start(bf16[34,1,128]{2,1,0:T(2,128)(2,1)S(1)} %get-tuple-element.60), channel_id=1, source_target_pairs={{1,0},{2,1},{3,2},{4,3},{5,4},{6,5},{7,6},{8,7},{9,8},{10,9},{11,1... | collective-permute-start | bytes 26120 | tf_op jit(solution)/shard_map/ppermute | solution.py:23
  430.2 21.9 %collective-permute-start.19 = (bf16[34,1,128]{2,1,0:T(2,128)(2,1)S(1)}, bf16[34,1,128]{2,1,0:T(2,128)(2,1)S(1)}, u32[]{:S(2)}, u32[]{:S(2)}) collective-permute-start(bf16[34,1,128]{2,1,0:T(2,128)(2,1)S(1)} %get-tuple-element.61), channel_id=1, source_target_pairs={{0,1},{1,2},{2,3},{3,4},{4,5},{5,6},{6,7},{7,8},{8,9},{9,10},{10,1... | collective-permute-start | bytes 26120 | tf_op jit(solution)/shard_map/ppermute | solution.py:22
  434.3 7.0 %collective-permute-start.10 = (bf16[34,1,128]{2,1,0:T(2,128)(2,1)S(1)}, bf16[34,1,128]{2,1,0:T(2,128)(2,1)S(1)}, u32[]{:S(2)}, u32[]{:S(2)}) collective-permute-start(bf16[34,1,128]{2,1,0:T(2,128)(2,1)S(1)} %get-tuple-element.69), channel_id=1, source_target_pairs={{0,1},{1,2},{2,3},{3,4},{4,5},{5,6},{6,7},{7,8},{8,9},{9,10},{10,1... | collective-permute-start | bytes 26120 | tf_op jit(solution)/shard_map/ppermute | solution.py:22
  436.7 6.6 %collective-permute-start.11 = (bf16[34,1,128]{2,1,0:T(2,128)(2,1)S(1)}, bf16[34,1,128]{2,1,0:T(2,128)(2,1)S(1)}, u32[]{:S(2)}, u32[]{:S(2)}) collective-permute-start(bf16[34,1,128]{2,1,0:T(2,128)(2,1)S(1)} %get-tuple-element.70), channel_id=1, source_target_pairs={{1,0},{2,1},{3,2},{4,3},{5,4},{6,5},{7,6},{8,7},{9,8},{10,9},{11,1... | collective-permute-start | bytes 26120 | tf_op jit(solution)/shard_map/ppermute | solution.py:23
  (38 other events, 331.5 us)
Sparse Core Ops, SparseCore 0:
  463.8 149.6 all-reduce.9
where the time goes:
time: 625 us; the launch traced here: 623 us
  blocking collectives  326 us (52%)
  waiting for transfers between devices  153 us (24%)
  starting transfers between devices  54.4 us (9%)
  matrix products  44.5 us (7%)
  between operations  16 us (3%)
  local copies, waits for them, and re-layouts  15.5 us (2%)
  other arithmetic  12.8 us (2%)
    psum x1, waiting for transfers between devices, per_device(): lax.psum((first_local, second_local), ('rows', 'cols'))  144 us
    psum x1, blocking collectives, per_device(): lax.psum((feature_sums, member_counts), ('rows', 'cols'))  68.6 us
    psum x1, blocking collectives, per_device(): lax.psum((jnp.sum(normed_grad, 0), jnp.sum(normed_grad * normed_act, 0)),...  63.3 us
    psum x1, blocking collectives, per_device(): lax.psum((jnp.sum(first_act, 0), jnp.sum(first_act * first_act, 0)), ('ro...  61.8 us
    unnamed x1, blocking collectives  60.8 us
    all_gather x2, blocking collectives, band_conv(): gathered = lax.all_gather(band_field, 'cols', axis=2, tiled=True)  58.3 us
    ppermute x10, starting transfers between devices, padded_2(): before = lax.ppermute(last, axis, up)  34.6 us
    ppermute x10, starting transfers between devices, padded_2(): after = lax.ppermute(initial, axis, down)  19.8 us
  transfers between devices with their start and end apart: 21, of which 5 were waited for; matrix products, arithmetic and copies ran while one was open for 5% of the time, Pallas kernels for 0%

commit v1 on v0

v1 whole, which is shorter than its diff:
```python
import functools
import math

import jax
import jax.numpy as jnp
from jax import lax
from jax.experimental import pallas as pl
from jax.experimental.pallas import tpu as pltpu
from jax.sharding import PartitionSpec as P

MESH = pl.DeviceIdType.MESH
HIGH = lax.Precision.HIGHEST
F32 = jnp.float32
BF16 = jnp.bfloat16
EPS = 1e-05
LABELS = 256
UP = 16
W = 80
DIRS = [(dr, dc) for dr in (-1, 0, 1) for dc in (-1, 0, 1) if (dr, dc) != (0, 0)]


def mm(a, b):
    return jnp.dot(a, b, preferred_element_type=F32)


def mm_t0(a, b, **kw):
    return lax.dot_general(a, b, (((0,), (0,)), ((), ())), preferred_element_type=F32, **kw)


def mm_t1(a, b, **kw):
    return lax.dot_general(a, b, (((1,), (1,)), ((), ())), preferred_element_type=F32, **kw)


def kernel(
    nr,
    nc,
    gin,
    gw1_hbm,
    gw2_hbm,
    pw,
    ein,
    imap,
    feats,
    iw,
    w1,
    w2,
    cot,
    enh_out,
    g1_out,
    g2_out,
    gg_out,
    gw1,
    gw2,
    gbuf,
    hbuf,
    hsend,
    xcat,
    zs,
    psend,
    precv,
    ssend,
    sbuf,
    gop,
    gos,
    gob,
    gobn,
    einp,
    cotp,
    pbuf,
    pall,
    nbp,
    ringp,
    fsend,
    fbuf,
    m3,
    a3,
    c3,
    cott,
    fgt,
    w2t,
    fa,
    ag,
    tsend,
    tcol,
    tsum,
    trow,
    gacc,
    gcol,
    gred,
    grow,
    gfin,
    gall,
    local_sem,
    col_s,
    col_r,
    nb_s,
    nb_r,
    part_s,
    part_r,
    row_s,
    row_r,
    go_s,
    go_r,
):
    r = lax.axis_index("rows")
    c = lax.axis_index("cols")

    def remote(src, dst, ss, rs, dev):
        return pltpu.make_async_remote_copy(
            src_ref=src, dst_ref=dst, send_sem=ss, recv_sem=rs, device_id=dev, device_id_type=MESH
        )

    def to_cols(n, src_of, dst, wait=False):
        def body(k, carry):
            t = lax.rem(c + k, nc)
            slot = t if wait else c
            copy = remote(src_of(t), dst(slot), col_s.at[n, t], col_r.at[n, slot], (r, t))
            copy.wait() if wait else copy.start()
            return carry

        lax.fori_loop(1, nc, body, 0)

    def to_rows(n, src, dst, wait=False):
        def body(k, carry):
            t = lax.rem(r + k, nr)
            slot = t if wait else r
            copy = remote(src, dst(slot), row_s.at[n, t], row_r.at[n, slot], (t, c))
            copy.wait() if wait else copy.start()
            return carry

        lax.fori_loop(1, nr, body, 0)

    def wrap_r(d):
        return lax.rem(r + d + nr, nr)

    def wrap_c(d):
        return lax.rem(c + d + nc, nc)

    own = [
        pltpu.make_async_copy(gw1_hbm, gw1, local_sem.at[0]),
        pltpu.make_async_copy(gw2_hbm, gw2, local_sem.at[1]),
        pltpu.make_async_copy(ein, einp.at[pl.ds(2, 32), pl.ds(8, 64)], local_sem.at[2]),
        pltpu.make_async_copy(cot, cotp.at[pl.ds(2, 32), pl.ds(8, 64)], local_sem.at[3]),
    ]
    for copy in own:
        copy.start()

    barrier = pltpu.get_barrier_semaphore()

    def greet(dr, dc):
        pl.semaphore_signal(barrier, inc=1, device_id=(wrap_r(dr), lax.rem(c + dc, nc)), device_id_type=MESH)

    def greet_cols(k, carry):
        @pl.when(k > 0)
        def _():
            greet(0, k)

        greet(1, k)
        greet(-1, k)
        return carry

    lax.fori_loop(0, nc, greet_cols, 0)
    for k in range(2, nr - 1):
        greet(k, 0)

    lane8 = lax.broadcasted_iota(jnp.int32, (8, 64), 1)
    row8 = lax.broadcasted_iota(jnp.int32, (8, 64), 0)
    packed = jnp.zeros((8, 16), F32)
    label = jnp.zeros((8, 1), F32)
    for br in range(2):
        strip = jnp.sum(feats[:, br * UP : (br + 1) * UP, :], axis=1)
        pick = ((lane8 // UP == row8 % 4) & (row8 // 4 == br)).astype(F32)
        packed = packed + mm_t1(pick, strip, precision=HIGH)
        corner = ((lane8 == UP * (row8 % 4)) & (row8 // 4 == br)).astype(F32)
        line = imap[br * UP : br * UP + 1, :].astype(F32)
        label = label + jnp.sum(corner * line, axis=1, keepdims=True)
    pbuf[...] = jnp.zeros_like(pbuf)
    pbuf[:, 0:16] = packed
    pbuf[:, 16:17] = jnp.full((8, 1), float(UP * UP), F32)
    pbuf[:, 17:18] = label

    pl.semaphore_wait(barrier, 3 * nc - 1 + nr - 3)

    to_cols(0, lambda t: gin, lambda s: gbuf.at[s])
    to_cols(1, lambda t: pbuf, lambda s: pall.at[s])

    def halo(i, d, src, dst):
        dr, dc = d
        rows_from = {-1: (0, 2), 0: (0, 32), 1: (30, 2)}[dr]
        rows_to = {-1: 34, 0: 2, 1: 0}[dr]
        cols_from = {-1: (0, 8), 0: (0, 64), 1: (56, 8)}[dc]
        cols_to = {-1: 72, 0: 8, 1: 0}[dc]
        n = (dr + 1) * 3 + dc + 1
        return remote(
            src.at[pl.ds(*rows_from), pl.ds(*cols_from)],
            dst.at[pl.ds(rows_to, rows_from[1]), pl.ds(cols_to, cols_from[1])],
            nb_s.at[i, n],
            nb_r.at[i, n],
            (wrap_r(dr), wrap_c(dc)),
        )

    def near(d):
        dr, dc = d
        n = (dr + 1) * 3 + dc + 1
        return remote(
            pbuf, nbp.at[1 - dr, 1 - dc], nb_s.at[2, n], nb_r.at[2, n], (wrap_r(dr), wrap_c(dc))
        )

    for d in DIRS:
        near(d).start()
    for d in DIRS:
        halo(1, d, cot, cotp).start()
    for d in DIRS:
        halo(0, d, ein, einp).start()

    gbuf[pl.ds(c, 1)] = gin[...][None]
    pall[pl.ds(c, 1)] = pbuf[...][None]
    nbp[1, 1] = pbuf[...]
    for a in range(3):
        for b in range(3):
            w2t[a, b * 128 : (b + 1) * 128, :] = (
                w2[2 - a, (2 - b) * 128 : (3 - b) * 128, :].astype(F32).T.astype(BF16)
            )

    col80 = lax.broadcasted_iota(jnp.int32, (W, 128), 0)
    colmap = ((col80 >= 8) | (c > 0)) & ((col80 < 72) | (c < nc - 1))
    colown = (col80 >= 8) & (col80 < 72)

    def spread(dst, i, value):
        dst[i, :, 0:128] = pltpu.roll(value, 1, 0).astype(BF16)
        dst[i, :, 128:256] = value.astype(BF16)
        dst[i, :, 256:384] = pltpu.roll(value, W - 1, 0).astype(BF16)

    def in_map(i, first, last):
        return colmap & ((i >= first) | (r > 0)) & ((i <= last) | (r < nr - 1))

    to_cols(1, lambda t: pbuf, lambda s: pall.at[s], wait=True)
    band_p = pall[...].reshape(8 * nc, 128)
    hot = (
        lax.broadcasted_iota(jnp.int32, (8 * nc, LABELS), 1) == band_p[:, 17:18].astype(jnp.int32)
    ).astype(F32)
    fsend[...] = mm_t0(band_p, hot, precision=HIGH)[0:24, :]
    to_rows(0, fsend, lambda s: fbuf.at[s])
    fbuf[pl.ds(r, 1)] = fsend[...][None]

    def band_conv(buf, w, n):
        for k in range(nc):
            xcat[:, k * 64 : (k + 1) * 64] = buf[k]
        x = xcat[...]
        j = lax.broadcasted_iota(jnp.int32, (128, 64), 0) % 64
        out = []
        for a in range(3):
            total = mm(x, w[a, 1])
            zs[8:136, :] = mm(x, w[a, 0])
            total = total + jnp.where(j > 0, zs[7:135, :], 0.0)
            zs[8:136, :] = mm(x, w[a, 2])
            total = total + jnp.where(j < 63, zs[9:137, :], 0.0)
            out.append(total)
        psend[n, 0] = out[2][0:64]
        psend[n, 1] = out[0][64:128]
        up = remote(psend.at[n, 0], precv.at[n, 1], part_s.at[n, 0], part_r.at[n, 1], (wrap_r(-1), c))
        down = remote(psend.at[n, 1], precv.at[n, 0], part_s.at[n, 1], part_r.at[n, 0], (wrap_r(1), c))
        up.start()
        down.start()
        top = out[1][0:64] + out[2][64:128]
        low = out[0][0:64] + out[1][64:128]
        up.wait()
        down.wait()
        top = top + jnp.where(r > 0, precv[n, 0], 0.0)
        low = low + jnp.where(r < nr - 1, precv[n, 1], 0.0)
        return jnp.concatenate([top, low], axis=0)

    zs[...] = jnp.zeros_like(zs)
    to_cols(0, lambda t: gin, lambda s: gbuf.at[s], wait=True)
    own[0].wait()
    first_raw = band_conv(gbuf, gw1, 0)
    ssend[...] = jnp.zeros_like(ssend)
    ssend[0:1, :] = jnp.sum(first_raw, 0, keepdims=True)
    ssend[1:2, :] = jnp.sum(first_raw * first_raw, 0, keepdims=True)
    to_rows(1, ssend, lambda s: sbuf.at[s])
    sbuf[pl.ds(r, 1)] = ssend[...][None]
    to_rows(1, ssend, lambda s: sbuf.at[s], wait=True)
    sums = jnp.sum(sbuf[...], axis=0)
    band_total = float(nr * 128)
    band_mean = sums[0:1, :] / band_total
    band_var = sums[1:2, :] / band_total - band_mean * band_mean
    normed = (first_raw - band_mean) * lax.rsqrt(band_var + EPS)
    hsend[...] = jnp.maximum(normed, 0.0).astype(BF16)
    to_cols(2, lambda t: hsend, lambda s: hbuf.at[s])
    hbuf[pl.ds(c, 1)] = hsend[...][None]

    own[3].wait()
    for d in DIRS:
        halo(1, d, cot, cotp).wait()

    def cot_row(i, carry):
        value = jnp.where(in_map(i, 2, 33), cotp[i].astype(F32), 0.0)
        spread(c3, i, value)
        return carry

    lax.fori_loop(0, 36, cot_row, 0)

    def cot_turn(i, carry):
        value = jnp.where(colown, cotp[i + 2].astype(F32), 0.0)
        cott[i] = value.T.astype(BF16)
        return carry

    lax.fori_loop(0, 32, cot_turn, 0)

    to_rows(0, fsend, lambda s: fbuf.at[s], wait=True)
    for d in DIRS:
        near(d).wait()
    fsum = jnp.sum(fbuf[...], axis=0)
    averages = fsum[0:16, :] / jnp.maximum(fsum[16:17, :], 1.0)
    ringp[...] = jnp.zeros_like(ringp)
    for br in range(4):
        dr, their_br = {0: (0, 1), 1: (1, 0), 2: (1, 1), 3: (2, 0)}[br]
        for q in range(6):
            dc, their_bc = (0, 3) if q == 0 else (2, 0) if q == 5 else (1, q - 1)
            p = their_br * 4 + their_bc
            ringp[br * 8 + q : br * 8 + q + 1, :] = nbp[dr, dc, p : p + 1, :]
    ring_hot = (
        lax.broadcasted_iota(jnp.int32, (32, LABELS), 1) == ringp[:, 17:18].astype(jnp.int32)
    ).astype(F32)
    ring_avg = mm_t1(ring_hot, averages, precision=HIGH)
    pooled = jnp.dot(ring_avg, iw[...], precision=HIGH, preferred_element_type=F32)

    to_cols(2, lambda t: hsend, lambda s: hbuf.at[s], wait=True)
    own[1].wait()
    second_raw = band_conv(hbuf, gw2, 1)
    global_out = (gin[...].astype(F32) + second_raw).astype(BF16).astype(F32)
    gop[...] = jnp.zeros_like(gop)
    gop[0, 8:72, :] = global_out[0:64]
    gop[1, 8:72, :] = global_out[64:128]
    for t in range(nc):
        for row in range(2):
            gos[t, row] = gop[row, 4 * t + 7 : 4 * t + 15, :]

    def go_copies(t, wait):
        slot = t if wait else c
        copies = [
            remote(gos.at[t, 0], gobn.at[1, slot], go_s.at[0, t], go_r.at[0, slot], (wrap_r(-1), t)),
            remote(gos.at[t, 1], gobn.at[0, slot], go_s.at[1, t], go_r.at[1, slot], (wrap_r(1), t)),
        ]
        for copy in copies:
            copy.wait() if wait else copy.start()

    to_cols(3, lambda t: gos.at[t], lambda s: gob.at[s])

    def go_start(k, carry):
        go_copies(lax.rem(c + k, nc), False)
        return carry

    def go_wait(k, carry):
        go_copies(lax.rem(c + k, nc), True)
        return carry

    lax.fori_loop(0, nc, go_start, 0)
    gob[pl.ds(c, 1)] = gos[pl.ds(c, 1)]
    own[2].wait()
    for d in DIRS:
        halo(0, d, ein, einp).wait()
    lax.fori_loop(0, nc, go_wait, 0)
    to_cols(3, lambda t: gos.at[t], lambda s: gob.at[s], wait=True)
    ring = jnp.zeros((32, 128), F32)
    for k in range(nc):
        rows = jnp.concatenate([gobn[0, k], gob[k, 0], gob[k, 1], gobn[1, k]], axis=0)
        ring = ring + mm(rows.astype(BF16), pw[k * 64 : (k + 1) * 64, :])
    terms = ring.astype(BF16).astype(F32) + pooled

    def mix_rows(br, start, stop):
        pieces = []
        for q in range(6):
            line = terms[br * 8 + q : br * 8 + q + 1, :]
            pieces.append(jnp.broadcast_to(line, (8 if q in (0, 5) else UP, 128)))
        add = jnp.concatenate(pieces, axis=0)

        def mix_row(i, carry):
            value = einp[i].astype(F32) + add
            value = jnp.where(in_map(i, 2, 33), value, 0.0).astype(BF16).astype(F32)
            spread(m3, i, value)
            return carry

        lax.fori_loop(start, stop, mix_row, 0)

    mix_rows(0, 0, 2)
    mix_rows(1, 2, 18)
    mix_rows(2, 18, 34)
    mix_rows(3, 34, 36)

    def conv_part(src, w, first, count):
        x = jnp.concatenate(
            [src[first + a : first + a + count].reshape(count * W, 384) for a in range(3)], axis=1
        )
        return mm(x, w[...].reshape(1152, 128)).reshape(count, W, 128)

    for half in range(2):
        fa[17 * half : 17 * half + 17] = conv_part(m3, w1, 17 * half, 17)

    def tile_sums(n, x, y):
        tsend[n] = jnp.zeros((8, 128), F32)
        tsend[n, 0:1, :] = jnp.sum(x, axis=(0, 1))[None]
        tsend[n, 1:2, :] = jnp.sum(y, axis=(0, 1))[None]
        to_cols(4 + n, lambda t: tsend.at[n], lambda s: tcol.at[n, s])
        tcol[n, pl.ds(c, 1)] = tsend[n][None]

    def tile_sums_2(n):
        to_cols(4 + n, lambda t: tsend.at[n], lambda s: tcol.at[n, s], wait=True)
        tsum[n] = jnp.sum(tcol[n], axis=0)
        to_rows(2 + n, tsum.at[n], lambda s: trow.at[n, s])
        trow[n, pl.ds(r, 1)] = tsum[n][None]

    def tile_sums_3(n):
        to_rows(2 + n, tsum.at[n], lambda s: trow.at[n, s], wait=True)
        return jnp.sum(trow[n], axis=0)

    act = fa[1:33, 8:72, :]
    tile_sums(0, act, act * act)
    ag[0:17] = conv_part(c3, w2t, 0, 17)
    tile_sums_2(0)
    ag[17:34] = conv_part(c3, w2t, 17, 17)
    sums = tile_sums_3(0)
    pixels = float(nr * nc * 2048)
    act_mean = sums[0:1, :] / pixels
    inverse_dev = lax.rsqrt(sums[1:2, :] / pixels - act_mean * act_mean + EPS)

    def act_row(i, carry):
        na = (fa[i] - act_mean) * inverse_dev
        s = jax.nn.sigmoid(na)
        fa[i] = na
        ng = ag[i] * s * (1.0 + na * (1.0 - s))
        ag[i] = ng
        spread(a3, i, jnp.where(in_map(i, 1, 32), na * s, 0.0).astype(BF16).astype(F32))
        return carry

    lax.fori_loop(0, 34, act_row, 0)
    ng = ag[1:33, 8:72, :]
    tile_sums(1, ng, ng * fa[1:33, 8:72, :])

    def weight_part(n, turned, src, first):
        lhs = jnp.concatenate([turned[i] for i in range(32)], axis=1)
        for a in range(3):
            got = mm(lhs, src[first + a : first + a + 32].reshape(32 * W, 384))
            for b in range(3):
                gacc[n, a * 384 + b * 128 : a * 384 + (b + 1) * 128, :] = got[:, b * 128 : (b + 1) * 128].T

    chunk = 1152 // nc

    def piece(t):
        return pl.ds(pl.multiple_of(t * chunk, 8), chunk)

    def grad_1(n):
        to_cols(6 + n, lambda t: gacc.at[n, piece(t)], lambda s: gcol.at[n, s])
        gcol[n, pl.ds(c, 1)] = gacc[n, piece(c)][None]

    def grad_2(n):
        to_cols(6 + n, lambda t: gacc.at[n, piece(t)], lambda s: gcol.at[n, s], wait=True)
        gred[n] = jnp.sum(gcol[n], axis=0)
        to_rows(4 + n, gred.at[n], lambda s: grow.at[n, s])
        grow[n, pl.ds(r, 1)] = gred[n][None]

    def grad_3(n):
        to_rows(4 + n, gred.at[n], lambda s: grow.at[n, s], wait=True)
        gfin[n] = jnp.sum(grow[n], axis=0) * (1.0 / math.sqrt(pixels))
        to_cols(8 + n, lambda t: gfin.at[n], lambda s: gall.at[n, piece(s)])
        gall[n, piece(c)] = gfin[n]

    def grad_4(n, out):
        to_cols(8 + n, lambda t: gfin.at[n], lambda s: gall.at[n, piece(s)], wait=True)
        out[...] = gall[n]

    weight_part(1, cott, a3, 0)
    grad_1(1)
    tile_sums_2(1)
    for half in range(2):
        got = conv_part(a3, w2, 16 * half, 16)
        enh_out[16 * half : 16 * half + 16] = (
            m3[2 + 16 * half : 18 + 16 * half, 8:72, 128:256].astype(F32) + got[:, 8:72, :]
        ).astype(BF16)
    sums = tile_sums_3(1)
    grad_mean = sums[0:1, :] / pixels
    cross_mean = sums[1:2, :] / pixels
    grad_2(1)

    def grad_row(i, carry):
        fg = inverse_dev * (ag[i] - grad_mean - fa[i] * cross_mean)
        fg = jnp.where(in_map(i, 1, 32), fg, 0.0).astype(BF16).astype(F32)
        ag[i] = fg

        @pl.when((i > 0) & (i < 33))
        def _():
            fgt[i - 1] = jnp.where(colown, fg, 0.0).T.astype(BF16)

        return carry

    lax.fori_loop(0, 34, grad_row, 0)
    weight_part(0, fgt, m3, 1)
    grad_1(0)
    grad_3(1)

    rows24 = lax.broadcasted_iota(jnp.int32, (24, W), 0)
    cols24 = lax.broadcasted_iota(jnp.int32, (24, W), 1)
    left = UP * (rows24 % 8) + 9 - rows24 // 8
    window = ((cols24 >= left) & (cols24 < left + UP) & (rows24 % 8 < 4)).astype(F32)
    picked = [[], [], []]
    direct = []
    for br in range(2):
        total = jnp.sum(ag[UP * br + 1 : UP * br + 17], axis=0)
        below = total - ag[UP * br + 1] + ag[UP * br + 17]
        above = total - ag[UP * br + 16] + ag[UP * br]
        for a, strip in enumerate((below, total, above)):
            picked[a].append(jnp.dot(window, strip, precision=HIGH, preferred_element_type=F32))
        strip = jnp.sum(c3[UP * br + 2 : UP * br + 18, :, 128:256].astype(F32), axis=0)
        direct.append(jnp.dot(window, strip, precision=HIGH, preferred_element_type=F32)[8:16])
    result = jnp.concatenate(direct, axis=0)
    for a in range(3):
        for b in range(3):
            s_ab = jnp.concatenate([picked[a][br][8 * b : 8 * b + 8] for br in range(2)], axis=0)
            result = result + mm_t1(
                s_ab, w1[a, b * 128 : (b + 1) * 128, :].astype(F32), precision=HIGH
            )
    gg_out[0] = result[0:4] * (1.0 / UP)
    gg_out[1] = result[8:12] * (1.0 / UP)

    grad_2(0)
    grad_4(1, g2_out)
    grad_3(0)
    grad_4(0, g1_out)


def per_device(
    nr,
    nc,
    global_in,
    global_first,
    global_second,
    project_weight,
    enhancer_input,
    instance_map,
    encoder_features,
    instance_weight,
    enhancer_first,
    enhancer_second,
    output_cotangent,
):
    vm = pl.BlockSpec(memory_space=pltpu.VMEM)
    hbm = pl.BlockSpec(memory_space=pl.ANY)
    chunk = 1152 // nc
    dma = pltpu.SemaphoreType.DMA
    scratch = [
        pltpu.VMEM((3, 3, 1024, 64), BF16),
        pltpu.VMEM((3, 3, 1024, 64), BF16),
        pltpu.VMEM((nc, 128, 64), BF16),
        pltpu.VMEM((nc, 128, 64), BF16),
        pltpu.VMEM((128, 64), BF16),
        pltpu.VMEM((128, 1024), BF16),
        pltpu.VMEM((144, 64), F32),
        pltpu.VMEM((2, 2, 64, 64), F32),
        pltpu.VMEM((2, 2, 64, 64), F32),
        pltpu.VMEM((8, 64), F32),
        pltpu.VMEM((nr, 8, 64), F32),
        pltpu.VMEM((2, 80, 64), F32),
        pltpu.VMEM((nc, 2, 8, 64), F32),
        pltpu.VMEM((nc, 2, 8, 64), F32),
        pltpu.VMEM((2, nc, 8, 64), F32),
        pltpu.VMEM((36, W, 128), BF16),
        pltpu.VMEM((36, W, 128), BF16),
        pltpu.VMEM((8, 128), F32),
        pltpu.VMEM((nc, 8, 128), F32),
        pltpu.VMEM((3, 3, 8, 128), F32),
        pltpu.VMEM((32, 128), F32),
        pltpu.VMEM((24, LABELS), F32),
        pltpu.VMEM((nr, 24, LABELS), F32),
        pltpu.VMEM((36, W, 384), BF16),
        pltpu.VMEM((34, W, 384), BF16),
        pltpu.VMEM((36, W, 384), BF16),
        pltpu.VMEM((32, 128, W), BF16),
        pltpu.VMEM((32, 128, W), BF16),
        pltpu.VMEM((3, 384, 128), BF16),
        pltpu.VMEM((34, W, 128), F32),
        pltpu.VMEM((34, W, 128), F32),
        pltpu.VMEM((2, 8, 128), F32),
        pltpu.VMEM((2, nc, 8, 128), F32),
        pltpu.VMEM((2, 8, 128), F32),
        pltpu.VMEM((2, nr, 8, 128), F32),
        pltpu.VMEM((2, 1152, 128), F32),
        pltpu.VMEM((2, nc, chunk, 128), F32),
        pltpu.VMEM((2, chunk, 128), F32),
        pltpu.VMEM((2, nr, chunk, 128), F32),
        pltpu.VMEM((2, chunk, 128), F32),
        pltpu.VMEM((2, 1152, 128), F32),
        dma((4,)),
        dma((10, nc)),
        dma((10, nc)),
        dma((3, 9)),
        dma((3, 9)),
        dma((2, 2)),
        dma((2, 2)),
        dma((6, nr)),
        dma((6, nr)),
        dma((2, nc)),
        dma((2, nc)),
    ]
    enhanced, g1, g2, gg = pl.pallas_call(
        functools.partial(kernel, nr, nc),
        out_shape=(
            jax.ShapeDtypeStruct((32, 64, 128), BF16),
            jax.ShapeDtypeStruct((1152, 128), F32),
            jax.ShapeDtypeStruct((1152, 128), F32),
            jax.ShapeDtypeStruct((2, 4, 128), F32),
        ),
        in_specs=[vm, hbm, hbm, vm, hbm, vm, vm, vm, vm, vm, hbm],
        out_specs=(vm, vm, vm, vm),
        scratch_shapes=scratch,
        compiler_params=pltpu.CompilerParams(
            collective_id=0, has_side_effects=True, vmem_limit_bytes=56 * 1024 * 1024
        ),
    )(
        global_in.reshape(128, 64),
        global_first,
        global_second,
        project_weight,
        enhancer_input,
        instance_map,
        encoder_features,
        instance_weight,
        enhancer_first.reshape(3, 384, 128),
        enhancer_second.reshape(3, 384, 128),
        output_cotangent,
    )
    return (enhanced, g1.reshape(3, 3, 128, 128), g2.reshape(3, 3, 128, 128), gg)


def solution(mesh):
    nr, nc = mesh.shape["rows"], mesh.shape["cols"]
    return jax.shard_map(
        functools.partial(per_device, nr, nc),
        mesh=mesh,
        in_specs=(
            P("rows", None, "cols"),
            P(None, None, None, "cols"),
            P(None, None, None, "cols"),
            P(),
            P("rows", "cols", None),
            P("rows", "cols"),
            P(None, "rows", "cols"),
            P(),
            P(),
            P(),
            P("rows", "cols", None),
        ),
        out_specs=(P("rows", "cols", None), P(), P(), P("rows", "cols", None)),
        check_vma=False,
    )
```

time: 625 us -> 127 us (0.20)
  blocking collectives: 326 us -> 0 us
  waiting for transfers between devices: 153 us -> 0 us
  Pallas kernels: 0 us -> 114 us
  starting transfers between devices: 54.4 us -> 0 us
  matrix products: 44.5 us -> 0 us
  between operations: 16 us -> 0.67 us
  other arithmetic: 12.8 us -> 0 us
    psum x4 -> x0, blocking collectives: 207 us -> none  [the longest x1 68.6 us: per_device(): lax.psum((feature_sums, member_counts), ('rows', 'cols'))]
    psum x1 -> x0, waiting for transfers between devices: 144 us -> none  [per_device(): lax.psum((first_local, second_local), ('rows', 'cols'))]
    pallas_call x0 -> x1, Pallas kernels: none -> 114 us  [per_device(): pl.pallas_call(functools.partial(kernel, nr, nc), out_shape=(jax.ShapeDty...]
    unnamed x1 -> x0, blocking collectives: 60.8 us -> none
    all_gather x2 -> x0, blocking collectives: 58.3 us -> none  [band_conv(): gathered = lax.all_gather(band_field, 'cols', axis=2, tiled=True)]
    ppermute x20 -> x0, starting transfers between devices: 54.4 us -> none  [the longest x10 34.6 us: padded_2(): before = lax.ppermute(last, axis, up)]
    dot_general x76 -> x0, matrix products: 44.5 us -> none  [the longest x36 17.9 us: conv_taps(): jnp.dot(window.reshape(row_count * col_count, window.shape[2]), weight[ta...]
    ppermute x20 -> x0, waiting for transfers between devices: 9.64 us -> none  [the longest x10 9.62 us: padded_2(): after = lax.ppermute(initial, axis, down)]
  transfers between devices with their start and end apart: 21 -> 0, of which waited for: 5 -> 0; matrix products, arithmetic and copies ran while one was open for 5% -> 0% of each run, Pallas kernels for 0% -> 0%
where the time goes in v1:
time: 127 us
  Pallas kernels  114 us (90%)
  local copies, waits for them, and re-layouts  11.5 us (9%)
    pallas_call x1, Pallas kernels, per_device(): pl.pallas_call(functools.partial(kernel, nr, nc), out_shape=(jax.ShapeDty...  114 us
    unnamed x12, local copies, waits for them, and re-layouts  11.5 us

profile of v1, /device:TPU:1, one launch (start us, length us, event | category | flops | bytes accessed | tf_op | source)
XLA Modules:
  0.0 126.5 jit_solution(12942789535885392062)
XLA Ops:
  0.6 0.0 copy-start
  0.6 3.8 %copy.15.gw1_hbm = bf16[3,3,1024,64]{3,2,1,0:T(8,128)(2,1)} copy(bf16[3,3,1024,64]{2,3,1,0:T(8,128)(2,1)} %param.12) | data formatting | bytes 2359296 | tf_op args[1]
  4.5 0.0 copy-done
  4.5 2.4 %copy.16.gw2_hbm = bf16[3,3,1024,64]{3,2,1,0:T(8,128)(2,1)} copy(bf16[3,3,1024,64]{2,3,1,0:T(8,128)(2,1)S(1)} %copy-done) | data formatting | bytes 2359296 | tf_op args[2]
  6.9 114.4 %shard_map.138 = (bf16[32,64,128]{2,1,0:T(8,128)(2,1)}, f32[1152,128]{1,0:T(8,128)}, f32[1152,128]{1,0:T(8,128)}, f32[2,4,128]{2,1,0:T(4,128)}) custom-call(bf16[128,64]{1,0:T(8,128)(2,1)} %bitcast.9, bf16[3,3,1024,64]{3,2,1,0:T(8,128)(2,1)} %copy.15.gw1_hbm, bf16[3,3,1024,64]{3,2,1,0:T(8,128)(2,1)} %copy.16.gw2_hbm, bf16[1024,128]{1,0:T(8,128)(2,1)} %pw.1, ...), custom_call_target="tpu_custom_call" | custom-call | tf_op jit(solution)/shard_map/pallas_call | solution.py:604
  121.3 0.0 copy-start.1
  121.3 0.0 copy-start.2
  121.3 1.9 %copy.21 = bf16[32,64,128]{2,1,0:T(8,128)(2,1)} copy(bf16[32,64,128]{2,1,0:T(8,128)(2,1)} %get-tuple-element.16) | data formatting | bytes 1048576
  123.2 1.9 %copy.22 = f32[3,3,128,128]{3,2,1,0:T(8,128)} copy(f32[3,3,128,128]{3,2,1,0:T(8,128)} %bitcast.6) | data formatting | bytes 1179648
  125.1 0.0 copy-done.1
  125.1 0.8 copy.23
  125.9 0.0 copy-done.2
  125.9 0.6 copy.24
Async XLA Ops:
  0.6 3.8 %copy-start = (bf16[3,3,1024,64]{2,3,1,0:T(8,128)(2,1)S(1)}, bf16[3,3,1024,64]{2,3,1,0:T(8,128)(2,1)}, u32[]{:S(2)}) copy-start(bf16[3,3,1024,64]{2,3,1,0:T(8,128)(2,1)} %param.13) | copy-start | bytes 3538948
  121.3 3.9 %copy-start.1 = (f32[1152,128]{1,0:T(8,128)S(1)}, f32[1152,128]{1,0:T(8,128)}, u32[]{:S(2)}) copy-start(f32[1152,128]{1,0:T(8,128)} %get-tuple-element.10) | copy-start | bytes 1769476
  121.3 4.7 %copy-start.2 = (f32[2,4,128]{2,1,0:T(4,128)S(1)}, f32[2,4,128]{2,1,0:T(4,128)}, u32[]{:S(2)}) copy-start(f32[2,4,128]{2,1,0:T(4,128)} %get-tuple-element.19) | copy-start | bytes 12292
